TPU v7x, 256 devices: a whole 4x4x8 slice. The times are simulated.
256 devices in a mesh: tm: 64 (over z, x, core), col: 4 (over y).
Axes of the slice: x: 4, y: 4, z: 8, core: 2. Of those that a mesh axis runs over, the one named last changes fastest.
Arguments:
- couple: float32 [64, 1024, 1024], P('tm'), may hold values from -1 to 1
- free_term: float32 [64, 64, 1024], P('tm'), may hold values from -4 to 4
- slab_left: float32 [64, 4, 1024, 1024], P('tm', None, None, 'col'), may hold values from -0.125 to 0.125
- slab_right: float32 [64, 4, 1024, 1024], P('tm', None, None, 'col'), may hold values from -0.125 to 0.125
- arrow_rows: float32 [64, 64, 1024], P('tm', None, 'col'), may hold values from -0.0234375 to 0.0234375
- corner_base: float32 [64, 64], replicated, may hold values from -4 to 4
Outputs:
- boundary: float32 [64, 64, 1024], P('tm', None, 'col')
- slab_inverse: float32 [64, 4, 64, 1024], P('tm', None, None, 'col')
- corner: float32 [64, 64], replicated
All inputs are finite; a program needn't handle non-finite values.
Results may differ from a plain program's by a relative error of at most 0.00015.
Values sent between devices are 32-bit elements; how exact they have to be, the bound alone decides.
No kernel may reach another device: no remote copies, remote signals or barrier semaphores. Data moves between devices by JAX's collectives and lax.ppermute only.
A program may use at most 128 MiB of HBM per device.

v0:
```python
import jax
import jax.numpy as jnp
from jax import lax
from jax.sharding import PartitionSpec as P


def from_behind(array, axis, by):
    count = lax.axis_size(axis)
    pairs = [(i, i + by) for i in range(count) if 0 <= i + by < count]
    return lax.ppermute(array, axis, pairs)


def local(couple, free_term, slab_left, slab_right, arrow_rows, corner_base):
    highest = lax.Precision.HIGHEST
    transfer = couple[0]
    own_term = free_term[0]
    part_count = lax.axis_size("tm")
    col_count = lax.axis_size("col")
    col_index = lax.axis_index("col")
    col_width = transfer.shape[1] // col_count
    position = lax.axis_index("tm")

    def advance(counter, state):
        later_state = from_behind(state, "tm", -1)

        def update(incoming):
            return (
                jnp.dot(incoming, transfer, precision=highest, preferred_element_type=jnp.float32)
                + own_term
            )

        def keep_state(incoming):
            return state

        return lax.cond(part_count - 2 - position == counter, update, keep_state, later_state)

    boundary = lax.fori_loop(0, part_count - 1, advance, own_term)
    following = from_behind(boundary, "tm", -1)
    slab_blocks = jnp.einsum(
        "ab,kbc->kac", boundary, slab_left[0], precision=highest, preferred_element_type=jnp.float32
    )
    slab_blocks = slab_blocks + jnp.einsum(
        "ab,kbc->kac",
        following,
        slab_right[0],
        precision=highest,
        preferred_element_type=jnp.float32,
    )
    own_columns = lax.dynamic_slice_in_dim(boundary, col_index * col_width, col_width, 1)
    partial_value = jnp.dot(
        arrow_rows[0], own_columns.T, precision=highest, preferred_element_type=jnp.float32
    )
    corner = corner_base + lax.psum(partial_value, ("tm", "col"))
    return (own_columns[None], slab_blocks[None], corner)


def solution(mesh):
    placed = (
        P("tm", None, None),
        P("tm", None, None),
        P("tm", None, None, "col"),
        P("tm", None, None, "col"),
        P("tm", None, "col"),
        P(),
    )
    return jax.shard_map(
        local,
        mesh=mesh,
        in_specs=placed,
        out_specs=(P("tm", None, "col"), P("tm", None, None, "col"), P()),
        check_vma=False,
    )
```

profile of v0, /device:TPU:1, one launch (start us, length us, event | category | flops | bytes accessed | tf_op | source)
XLA Modules:
  0.0 790.8 jit_solution(10620637160481820337)
XLA Ops:
  1.6 669.1 %while.18 = (s32[]{:T(128)}, f32[64,1024]{1,0:T(8,128)S(1)}, s32[]{:T(128)}, f32[1024,1024]{1,0:T(8,128)}, f32[64,1024]{1,0:T(8,128)}, /*index=5*/s32[]{:T(128)}) while((s32[]{:T(128)}, f32[64,1024]{1,0:T(8,128)S(1)}, s32[]{:T(128)}, f32[1024,1024]{1,0:T(8,128)}, f32[64,1024]{1,0:T(8,128)}, /*index=5*/s32[]{:T(128)}) %tuple.60), condition=%wide.region_3.0_spmd, body=%wide.region_0.0_spmd.sunk | while | flops 805371904 | bytes 6029475 | solution.py:37
  114.0 7.9 collective-permute-done
  123.8 7.9 collective-permute-done
  133.5 7.9 collective-permute-done
  143.3 7.9 collective-permute-done
  153.1 7.9 collective-permute-done
  162.9 7.9 collective-permute-done
  172.7 7.9 collective-permute-done
  182.5 7.9 collective-permute-done
  192.3 7.9 collective-permute-done
  202.1 7.9 collective-permute-done
  211.9 7.9 collective-permute-done
  221.7 7.9 collective-permute-done
  231.4 7.9 collective-permute-done
  241.2 7.9 collective-permute-done
  251.0 7.9 collective-permute-done
  260.8 7.9 collective-permute-done
  270.6 7.9 collective-permute-done
  280.4 7.9 collective-permute-done
  290.2 7.9 collective-permute-done
  300.0 7.9 collective-permute-done
  309.8 7.9 collective-permute-done
  319.6 7.9 collective-permute-done
  329.3 7.9 collective-permute-done
  339.1 7.9 collective-permute-done
  348.9 7.9 collective-permute-done
  358.7 7.9 collective-permute-done
  368.5 7.9 collective-permute-done
  378.3 7.9 collective-permute-done
  388.1 7.9 collective-permute-done
  574.1 84.1 %collective-permute-done = f32[64,1024]{1,0:T(8,128)S(1)} collective-permute-done((f32[64,1024]{1,0:T(8,128)S(1)}, f32[64,1024]{1,0:T(8,128)S(1)}, u32[]{:S(2)}, u32[]{:S(2)}) %collective-permute-start) | collective-permute-done | bytes 262176 | tf_op jit(solution)/shard_map/while/body/eval_jaxpr/ppermute | solution.py:10
  674.2 107.5 %psum.7 = f32[64,64]{0,1:T(8,128)S(1)} all-reduce(f32[64,64]{0,1:T(8,128)S(1)} %convolution_bitcast_fusion), channel_id=1, replica_groups=mesh['tm'=64,'col'=4] {'tm','col'}, use_global_device_ids=true, to_apply=%region_4.0 | all-reduce | flops 4096 | bytes 32768 | tf_op jit(solution)/shard_map/psum | solution.py:53
  (176 shorter events, 374.3 us)
Async XLA Ops:
  112.0 9.8 %collective-permute-start = (f32[64,1024]{1,0:T(8,128)S(1)}, f32[64,1024]{1,0:T(8,128)S(1)}, u32[]{:S(2)}, u32[]{:S(2)}) collective-permute-start(f32[64,1024]{1,0:T(8,128)S(1)} %get-tuple-element.202), channel_id=1, source_target_pairs={{4,0},{8,4},{12,8},{16,12},{20,16},{24,20},{28,24},{32,28},{36,32}... | collective-permute-start | bytes 786440 | tf_op jit(solution)/shard_map/while/body/eval_jaxpr/ppermute | solution.py:10
  121.8 9.8 %collective-permute-start = (f32[64,1024]{1,0:T(8,128)S(1)}, f32[64,1024]{1,0:T(8,128)S(1)}, u32[]{:S(2)}, u32[]{:S(2)}) collective-permute-start(f32[64,1024]{1,0:T(8,128)S(1)} %get-tuple-element.202), channel_id=1, source_target_pairs={{4,0},{8,4},{12,8},{16,12},{20,16},{24,20},{28,24},{32,28},{36,32}... | collective-permute-start | bytes 786440 | tf_op jit(solution)/shard_map/while/body/eval_jaxpr/ppermute | solution.py:10
  131.6 9.8 %collective-permute-start = (f32[64,1024]{1,0:T(8,128)S(1)}, f32[64,1024]{1,0:T(8,128)S(1)}, u32[]{:S(2)}, u32[]{:S(2)}) collective-permute-start(f32[64,1024]{1,0:T(8,128)S(1)} %get-tuple-element.202), channel_id=1, source_target_pairs={{4,0},{8,4},{12,8},{16,12},{20,16},{24,20},{28,24},{32,28},{36,32}... | collective-permute-start | bytes 786440 | tf_op jit(solution)/shard_map/while/body/eval_jaxpr/ppermute | solution.py:10
  141.4 9.8 %collective-permute-start = (f32[64,1024]{1,0:T(8,128)S(1)}, f32[64,1024]{1,0:T(8,128)S(1)}, u32[]{:S(2)}, u32[]{:S(2)}) collective-permute-start(f32[64,1024]{1,0:T(8,128)S(1)} %get-tuple-element.202), channel_id=1, source_target_pairs={{4,0},{8,4},{12,8},{16,12},{20,16},{24,20},{28,24},{32,28},{36,32}... | collective-permute-start | bytes 786440 | tf_op jit(solution)/shard_map/while/body/eval_jaxpr/ppermute | solution.py:10
  151.2 9.8 %collective-permute-start = (f32[64,1024]{1,0:T(8,128)S(1)}, f32[64,1024]{1,0:T(8,128)S(1)}, u32[]{:S(2)}, u32[]{:S(2)}) collective-permute-start(f32[64,1024]{1,0:T(8,128)S(1)} %get-tuple-element.202), channel_id=1, source_target_pairs={{4,0},{8,4},{12,8},{16,12},{20,16},{24,20},{28,24},{32,28},{36,32}... | collective-permute-start | bytes 786440 | tf_op jit(solution)/shard_map/while/body/eval_jaxpr/ppermute | solution.py:10
  161.0 9.8 %collective-permute-start = (f32[64,1024]{1,0:T(8,128)S(1)}, f32[64,1024]{1,0:T(8,128)S(1)}, u32[]{:S(2)}, u32[]{:S(2)}) collective-permute-start(f32[64,1024]{1,0:T(8,128)S(1)} %get-tuple-element.202), channel_id=1, source_target_pairs={{4,0},{8,4},{12,8},{16,12},{20,16},{24,20},{28,24},{32,28},{36,32}... | collective-permute-start | bytes 786440 | tf_op jit(solution)/shard_map/while/body/eval_jaxpr/ppermute | solution.py:10
  170.8 9.8 %collective-permute-start = (f32[64,1024]{1,0:T(8,128)S(1)}, f32[64,1024]{1,0:T(8,128)S(1)}, u32[]{:S(2)}, u32[]{:S(2)}) collective-permute-start(f32[64,1024]{1,0:T(8,128)S(1)} %get-tuple-element.202), channel_id=1, source_target_pairs={{4,0},{8,4},{12,8},{16,12},{20,16},{24,20},{28,24},{32,28},{36,32}... | collective-permute-start | bytes 786440 | tf_op jit(solution)/shard_map/while/body/eval_jaxpr/ppermute | solution.py:10
  180.6 9.8 %collective-permute-start = (f32[64,1024]{1,0:T(8,128)S(1)}, f32[64,1024]{1,0:T(8,128)S(1)}, u32[]{:S(2)}, u32[]{:S(2)}) collective-permute-start(f32[64,1024]{1,0:T(8,128)S(1)} %get-tuple-element.202), channel_id=1, source_target_pairs={{4,0},{8,4},{12,8},{16,12},{20,16},{24,20},{28,24},{32,28},{36,32}... | collective-permute-start | bytes 786440 | tf_op jit(solution)/shard_map/while/body/eval_jaxpr/ppermute | solution.py:10
  190.4 9.8 %collective-permute-start = (f32[64,1024]{1,0:T(8,128)S(1)}, f32[64,1024]{1,0:T(8,128)S(1)}, u32[]{:S(2)}, u32[]{:S(2)}) collective-permute-start(f32[64,1024]{1,0:T(8,128)S(1)} %get-tuple-element.202), channel_id=1, source_target_pairs={{4,0},{8,4},{12,8},{16,12},{20,16},{24,20},{28,24},{32,28},{36,32}... | collective-permute-start | bytes 786440 | tf_op jit(solution)/shard_map/while/body/eval_jaxpr/ppermute | solution.py:10
  200.2 9.8 %collective-permute-start = (f32[64,1024]{1,0:T(8,128)S(1)}, f32[64,1024]{1,0:T(8,128)S(1)}, u32[]{:S(2)}, u32[]{:S(2)}) collective-permute-start(f32[64,1024]{1,0:T(8,128)S(1)} %get-tuple-element.202), channel_id=1, source_target_pairs={{4,0},{8,4},{12,8},{16,12},{20,16},{24,20},{28,24},{32,28},{36,32}... | collective-permute-start | bytes 786440 | tf_op jit(solution)/shard_map/while/body/eval_jaxpr/ppermute | solution.py:10
  209.9 9.8 %collective-permute-start = (f32[64,1024]{1,0:T(8,128)S(1)}, f32[64,1024]{1,0:T(8,128)S(1)}, u32[]{:S(2)}, u32[]{:S(2)}) collective-permute-start(f32[64,1024]{1,0:T(8,128)S(1)} %get-tuple-element.202), channel_id=1, source_target_pairs={{4,0},{8,4},{12,8},{16,12},{20,16},{24,20},{28,24},{32,28},{36,32}... | collective-permute-start | bytes 786440 | tf_op jit(solution)/shard_map/while/body/eval_jaxpr/ppermute | solution.py:10
  219.7 9.8 %collective-permute-start = (f32[64,1024]{1,0:T(8,128)S(1)}, f32[64,1024]{1,0:T(8,128)S(1)}, u32[]{:S(2)}, u32[]{:S(2)}) collective-permute-start(f32[64,1024]{1,0:T(8,128)S(1)} %get-tuple-element.202), channel_id=1, source_target_pairs={{4,0},{8,4},{12,8},{16,12},{20,16},{24,20},{28,24},{32,28},{36,32}... | collective-permute-start | bytes 786440 | tf_op jit(solution)/shard_map/while/body/eval_jaxpr/ppermute | solution.py:10
  229.5 9.8 %collective-permute-start = (f32[64,1024]{1,0:T(8,128)S(1)}, f32[64,1024]{1,0:T(8,128)S(1)}, u32[]{:S(2)}, u32[]{:S(2)}) collective-permute-start(f32[64,1024]{1,0:T(8,128)S(1)} %get-tuple-element.202), channel_id=1, source_target_pairs={{4,0},{8,4},{12,8},{16,12},{20,16},{24,20},{28,24},{32,28},{36,32}... | collective-permute-start | bytes 786440 | tf_op jit(solution)/shard_map/while/body/eval_jaxpr/ppermute | solution.py:10
  239.3 9.8 %collective-permute-start = (f32[64,1024]{1,0:T(8,128)S(1)}, f32[64,1024]{1,0:T(8,128)S(1)}, u32[]{:S(2)}, u32[]{:S(2)}) collective-permute-start(f32[64,1024]{1,0:T(8,128)S(1)} %get-tuple-element.202), channel_id=1, source_target_pairs={{4,0},{8,4},{12,8},{16,12},{20,16},{24,20},{28,24},{32,28},{36,32}... | collective-permute-start | bytes 786440 | tf_op jit(solution)/shard_map/while/body/eval_jaxpr/ppermute | solution.py:10
  249.1 9.8 %collective-permute-start = (f32[64,1024]{1,0:T(8,128)S(1)}, f32[64,1024]{1,0:T(8,128)S(1)}, u32[]{:S(2)}, u32[]{:S(2)}) collective-permute-start(f32[64,1024]{1,0:T(8,128)S(1)} %get-tuple-element.202), channel_id=1, source_target_pairs={{4,0},{8,4},{12,8},{16,12},{20,16},{24,20},{28,24},{32,28},{36,32}... | collective-permute-start | bytes 786440 | tf_op jit(solution)/shard_map/while/body/eval_jaxpr/ppermute | solution.py:10
  258.9 9.8 %collective-permute-start = (f32[64,1024]{1,0:T(8,128)S(1)}, f32[64,1024]{1,0:T(8,128)S(1)}, u32[]{:S(2)}, u32[]{:S(2)}) collective-permute-start(f32[64,1024]{1,0:T(8,128)S(1)} %get-tuple-element.202), channel_id=1, source_target_pairs={{4,0},{8,4},{12,8},{16,12},{20,16},{24,20},{28,24},{32,28},{36,32}... | collective-permute-start | bytes 786440 | tf_op jit(solution)/shard_map/while/body/eval_jaxpr/ppermute | solution.py:10
  268.7 9.8 %collective-permute-start = (f32[64,1024]{1,0:T(8,128)S(1)}, f32[64,1024]{1,0:T(8,128)S(1)}, u32[]{:S(2)}, u32[]{:S(2)}) collective-permute-start(f32[64,1024]{1,0:T(8,128)S(1)} %get-tuple-element.202), channel_id=1, source_target_pairs={{4,0},{8,4},{12,8},{16,12},{20,16},{24,20},{28,24},{32,28},{36,32}... | collective-permute-start | bytes 786440 | tf_op jit(solution)/shard_map/while/body/eval_jaxpr/ppermute | solution.py:10
  278.5 9.8 %collective-permute-start = (f32[64,1024]{1,0:T(8,128)S(1)}, f32[64,1024]{1,0:T(8,128)S(1)}, u32[]{:S(2)}, u32[]{:S(2)}) collective-permute-start(f32[64,1024]{1,0:T(8,128)S(1)} %get-tuple-element.202), channel_id=1, source_target_pairs={{4,0},{8,4},{12,8},{16,12},{20,16},{24,20},{28,24},{32,28},{36,32}... | collective-permute-start | bytes 786440 | tf_op jit(solution)/shard_map/while/body/eval_jaxpr/ppermute | solution.py:10
  288.3 9.8 %collective-permute-start = (f32[64,1024]{1,0:T(8,128)S(1)}, f32[64,1024]{1,0:T(8,128)S(1)}, u32[]{:S(2)}, u32[]{:S(2)}) collective-permute-start(f32[64,1024]{1,0:T(8,128)S(1)} %get-tuple-element.202), channel_id=1, source_target_pairs={{4,0},{8,4},{12,8},{16,12},{20,16},{24,20},{28,24},{32,28},{36,32}... | collective-permute-start | bytes 786440 | tf_op jit(solution)/shard_map/while/body/eval_jaxpr/ppermute | solution.py:10
  298.1 9.8 %collective-permute-start = (f32[64,1024]{1,0:T(8,128)S(1)}, f32[64,1024]{1,0:T(8,128)S(1)}, u32[]{:S(2)}, u32[]{:S(2)}) collective-permute-start(f32[64,1024]{1,0:T(8,128)S(1)} %get-tuple-element.202), channel_id=1, source_target_pairs={{4,0},{8,4},{12,8},{16,12},{20,16},{24,20},{28,24},{32,28},{36,32}... | collective-permute-start | bytes 786440 | tf_op jit(solution)/shard_map/while/body/eval_jaxpr/ppermute | solution.py:10
  307.8 9.8 %collective-permute-start = (f32[64,1024]{1,0:T(8,128)S(1)}, f32[64,1024]{1,0:T(8,128)S(1)}, u32[]{:S(2)}, u32[]{:S(2)}) collective-permute-start(f32[64,1024]{1,0:T(8,128)S(1)} %get-tuple-element.202), channel_id=1, source_target_pairs={{4,0},{8,4},{12,8},{16,12},{20,16},{24,20},{28,24},{32,28},{36,32}... | collective-permute-start | bytes 786440 | tf_op jit(solution)/shard_map/while/body/eval_jaxpr/ppermute | solution.py:10
  317.6 9.8 %collective-permute-start = (f32[64,1024]{1,0:T(8,128)S(1)}, f32[64,1024]{1,0:T(8,128)S(1)}, u32[]{:S(2)}, u32[]{:S(2)}) collective-permute-start(f32[64,1024]{1,0:T(8,128)S(1)} %get-tuple-element.202), channel_id=1, source_target_pairs={{4,0},{8,4},{12,8},{16,12},{20,16},{24,20},{28,24},{32,28},{36,32}... | collective-permute-start | bytes 786440 | tf_op jit(solution)/shard_map/while/body/eval_jaxpr/ppermute | solution.py:10
  327.4 9.8 %collective-permute-start = (f32[64,1024]{1,0:T(8,128)S(1)}, f32[64,1024]{1,0:T(8,128)S(1)}, u32[]{:S(2)}, u32[]{:S(2)}) collective-permute-start(f32[64,1024]{1,0:T(8,128)S(1)} %get-tuple-element.202), channel_id=1, source_target_pairs={{4,0},{8,4},{12,8},{16,12},{20,16},{24,20},{28,24},{32,28},{36,32}... | collective-permute-start | bytes 786440 | tf_op jit(solution)/shard_map/while/body/eval_jaxpr/ppermute | solution.py:10
  337.2 9.8 %collective-permute-start = (f32[64,1024]{1,0:T(8,128)S(1)}, f32[64,1024]{1,0:T(8,128)S(1)}, u32[]{:S(2)}, u32[]{:S(2)}) collective-permute-start(f32[64,1024]{1,0:T(8,128)S(1)} %get-tuple-element.202), channel_id=1, source_target_pairs={{4,0},{8,4},{12,8},{16,12},{20,16},{24,20},{28,24},{32,28},{36,32}... | collective-permute-start | bytes 786440 | tf_op jit(solution)/shard_map/while/body/eval_jaxpr/ppermute | solution.py:10
  347.0 9.8 %collective-permute-start = (f32[64,1024]{1,0:T(8,128)S(1)}, f32[64,1024]{1,0:T(8,128)S(1)}, u32[]{:S(2)}, u32[]{:S(2)}) collective-permute-start(f32[64,1024]{1,0:T(8,128)S(1)} %get-tuple-element.202), channel_id=1, source_target_pairs={{4,0},{8,4},{12,8},{16,12},{20,16},{24,20},{28,24},{32,28},{36,32}... | collective-permute-start | bytes 786440 | tf_op jit(solution)/shard_map/while/body/eval_jaxpr/ppermute | solution.py:10
  356.8 9.8 %collective-permute-start = (f32[64,1024]{1,0:T(8,128)S(1)}, f32[64,1024]{1,0:T(8,128)S(1)}, u32[]{:S(2)}, u32[]{:S(2)}) collective-permute-start(f32[64,1024]{1,0:T(8,128)S(1)} %get-tuple-element.202), channel_id=1, source_target_pairs={{4,0},{8,4},{12,8},{16,12},{20,16},{24,20},{28,24},{32,28},{36,32}... | collective-permute-start | bytes 786440 | tf_op jit(solution)/shard_map/while/body/eval_jaxpr/ppermute | solution.py:10
  366.6 9.8 %collective-permute-start = (f32[64,1024]{1,0:T(8,128)S(1)}, f32[64,1024]{1,0:T(8,128)S(1)}, u32[]{:S(2)}, u32[]{:S(2)}) collective-permute-start(f32[64,1024]{1,0:T(8,128)S(1)} %get-tuple-element.202), channel_id=1, source_target_pairs={{4,0},{8,4},{12,8},{16,12},{20,16},{24,20},{28,24},{32,28},{36,32}... | collective-permute-start | bytes 786440 | tf_op jit(solution)/shard_map/while/body/eval_jaxpr/ppermute | solution.py:10
  376.4 9.8 %collective-permute-start = (f32[64,1024]{1,0:T(8,128)S(1)}, f32[64,1024]{1,0:T(8,128)S(1)}, u32[]{:S(2)}, u32[]{:S(2)}) collective-permute-start(f32[64,1024]{1,0:T(8,128)S(1)} %get-tuple-element.202), channel_id=1, source_target_pairs={{4,0},{8,4},{12,8},{16,12},{20,16},{24,20},{28,24},{32,28},{36,32}... | collective-permute-start | bytes 786440 | tf_op jit(solution)/shard_map/while/body/eval_jaxpr/ppermute | solution.py:10
  386.2 9.8 %collective-permute-start = (f32[64,1024]{1,0:T(8,128)S(1)}, f32[64,1024]{1,0:T(8,128)S(1)}, u32[]{:S(2)}, u32[]{:S(2)}) collective-permute-start(f32[64,1024]{1,0:T(8,128)S(1)} %get-tuple-element.202), channel_id=1, source_target_pairs={{4,0},{8,4},{12,8},{16,12},{20,16},{24,20},{28,24},{32,28},{36,32}... | collective-permute-start | bytes 786440 | tf_op jit(solution)/shard_map/while/body/eval_jaxpr/ppermute | solution.py:10
  396.0 9.8 %collective-permute-start = (f32[64,1024]{1,0:T(8,128)S(1)}, f32[64,1024]{1,0:T(8,128)S(1)}, u32[]{:S(2)}, u32[]{:S(2)}) collective-permute-start(f32[64,1024]{1,0:T(8,128)S(1)} %get-tuple-element.202), channel_id=1, source_target_pairs={{4,0},{8,4},{12,8},{16,12},{20,16},{24,20},{28,24},{32,28},{36,32}... | collective-permute-start | bytes 786440 | tf_op jit(solution)/shard_map/while/body/eval_jaxpr/ppermute | solution.py:10
  572.2 86.0 %collective-permute-start = (f32[64,1024]{1,0:T(8,128)S(1)}, f32[64,1024]{1,0:T(8,128)S(1)}, u32[]{:S(2)}, u32[]{:S(2)}) collective-permute-start(f32[64,1024]{1,0:T(8,128)S(1)} %get-tuple-element.202), channel_id=1, source_target_pairs={{4,0},{8,4},{12,8},{16,12},{20,16},{24,20},{28,24},{32,28},{36,32}... | collective-permute-start | bytes 786440 | tf_op jit(solution)/shard_map/while/body/eval_jaxpr/ppermute | solution.py:10
  670.7 116.7 %collective-permute-start.1 = (f32[64,1024]{1,0:T(8,128)S(1)}, f32[64,1024]{1,0:T(8,128)S(1)}, u32[]{:S(2)}, u32[]{:S(2)}) collective-permute-start(f32[64,1024]{1,0:T(8,128)S(1)} %get-tuple-element.150), channel_id=1, source_target_pairs={{4,0},{8,4},{12,8},{16,12},{20,16},{24,20},{28,24},{32,28},{36,32}... | collective-permute-start | bytes 786440 | tf_op jit(solution)/shard_map/ppermute | solution.py:10
  (35 other events, 1635.1 us)
where the time goes:
time: 793 us; the launch traced here: 791 us
  waiting for transfers between devices  540 us (68%)
  starting transfers between devices  126 us (16%)
  blocking collectives  108 us (14%)
  matrix products  13.4 us (2%)
    ppermute x64, waiting for transfers between devices, from_behind(): return lax.ppermute(array, axis, pairs)  540 us
    ppermute x64, starting transfers between devices, from_behind(): return lax.ppermute(array, axis, pairs)  126 us
    psum x1, blocking collectives, local(): corner = corner_base + lax.psum(partial_value, ('tm', 'col'))  108 us
  transfers between devices with their start and end apart: 64, of which 63 were waited for; matrix products, arithmetic and copies ran while one was open for 1% of the time, Pallas kernels for 0%

commit v1 on v0

v1 whole, which is shorter than its diff:
```python
import functools
import jax
import jax.numpy as jnp
from jax import lax
from jax.experimental import pallas as pl
from jax.experimental.pallas import tpu as pltpu
from jax.sharding import PartitionSpec as P

PARTS = 64
N = 1024
COLS = 4
ROWS = 16
BLOCK = 256
TOP = 20
GROUPS = (PARTS - TOP) // 4
F32 = jnp.float32
BF16 = jnp.bfloat16
VMEM = pl.BlockSpec(memory_space=pltpu.VMEM)
SMEM = pl.BlockSpec(memory_space=pltpu.SMEM)


def split(value):
    high = value.astype(BF16)
    return high, (value - high.astype(F32)).astype(BF16)


def product(left, high, low):
    rows = left.shape[0]
    left_high, left_low = split(left)
    both = jnp.dot(jnp.concatenate([left_high, left_low], 0), high, preferred_element_type=F32)
    return both[:rows] + both[rows:] + jnp.dot(left_high, low, preferred_element_type=F32)


def call(body, outs, specs, operands, flops=0, limit=8, **kw):
    return pl.pallas_call(
        body,
        out_shape=outs,
        in_specs=specs,
        out_specs=[VMEM] * len(outs),
        compiler_params=pltpu.CompilerParams(vmem_limit_bytes=limit << 20),
        cost_estimate=pl.CostEstimate(flops=flops, bytes_accessed=4 << 20, transcendentals=0),
        **kw,
    )(*operands)


def shape(*dims, dtype=F32):
    return jax.ShapeDtypeStruct(dims, dtype)


def tall_body(left_ref, bias_ref, high_ref, low_ref, out_ref):
    out_ref[...] = product(left_ref[...], high_ref[...], low_ref[...])
    out_ref[BLOCK:, :] += bias_ref[...]


def tall(left, bias, high, low):
    (out,) = call(tall_body, [shape(BLOCK + ROWS, N)], [VMEM] * 4, (left, bias, high, low), 6 * 272 * N * N)
    return out


def keep_or(meta_ref, test, run, states_in, states_out):
    active = test(meta_ref[0])

    @pl.when(active)
    def _():
        run()

    @pl.when(jnp.logical_not(active))
    def _():
        for before, after in zip(states_in, states_out):
            after[...] = before[...]


def two_body(test, meta, got, in_0, odd_0, even_0, fo, fe, oh, ol, eh, el, in_1, odd_1, even_1):
    def run():
        x = got[...]
        odd = product(x, oh[...], ol[...]) + fo[...]
        in_1[...] = x
        odd_1[...] = odd
        even_1[...] = product(odd, eh[...], el[...]) + fe[...]

    keep_or(meta, test, run, (in_0, odd_0, even_0), (in_1, odd_1, even_1))


def two_steps(test, meta, got, states, terms, mats):
    return call(
        functools.partial(two_body, test),
        [shape(ROWS, N)] * 3,
        [SMEM] + [VMEM] * 10,
        (meta, got, *states, *terms, *mats),
        12 * 16 * N * N,
        input_output_aliases={2: 0, 3: 1, 4: 2},
    )


def one_body(test, meta, got, in_0, state_0, term, high, low, in_1, state_1):
    def run():
        x = got[...]
        in_1[...] = x
        state_1[...] = product(x, high[...], low[...]) + term[...]

    keep_or(meta, test, run, (in_0, state_0), (in_1, state_1))


def one_step(test, meta, got, states, term, mats):
    return call(
        functools.partial(one_body, test),
        [shape(ROWS, N)] * 2,
        [SMEM] + [VMEM] * 6,
        (meta, got, *states, term, *mats),
        6 * 16 * N * N,
        input_output_aliases={2: 0, 3: 1},
    )


def place_body(place_ref, b0, b1, b2, b3, high_ref, low_ref):
    for index, block in enumerate((b0, b1, b2, b3)):
        high, low = split(block[...])
        at = pl.ds(pl.multiple_of(place_ref[1 + index] * BLOCK, BLOCK), BLOCK)
        high_ref[at, :] = high
        low_ref[at, :] = low


def slab_body(place_ref, b0, b1, b2, b3, lh, ll, rh, rl, x_ref, out_ref, next_ref):
    for index, block in enumerate((b0, b1, b2, b3)):
        at = pl.ds(pl.multiple_of(place_ref[1 + index] * ROWS, ROWS), ROWS)
        x_ref[at, :] = block[:ROWS, :]
        next_ref[at, :] = block[ROWS:, :]
    own = x_ref[...]
    later = next_ref[...]
    for k in range(4):
        out_ref[k] = product(own, lh[k * N : k * N + N, :], ll[k * N : k * N + N, :])
        out_ref[k] += product(later, rh[k * N : k * N + N, :], rl[k * N : k * N + N, :])


def split_body(value_ref, high_ref, low_ref):
    high_ref[...], low_ref[...] = split(value_ref[...])


def halves(value):
    rows, columns = value.shape
    tile = pl.BlockSpec((BLOCK, columns), lambda i: (i, 0))
    return pl.pallas_call(
        split_body,
        grid=(rows // BLOCK,),
        out_shape=[shape(rows, columns, dtype=BF16)] * 2,
        in_specs=[tile],
        out_specs=[tile, tile],
        compiler_params=pltpu.CompilerParams(vmem_limit_bytes=8 << 20),
        cost_estimate=pl.CostEstimate(flops=2 * rows * columns, bytes_accessed=8 * rows * columns, transcendentals=0),
    )(value)


def around(value, members):
    return [lax.ppermute(value, ("tm", "col"), [(t * COLS + j, t * COLS + (j + by) % COLS) for t in members for j in range(COLS)]) for by in (1, 3, 2)]


def local(couple, free_term, slab_left, slab_right, arrow_rows, corner_base):
    me = lax.axis_index("tm")
    c = lax.axis_index("col")
    own = couple[0]
    meta = jnp.stack([me, c, (c + 3) % COLS, (c + 1) % COLS, (c + 2) % COLS]).astype(jnp.int32)
    f = lax.dynamic_slice_in_dim(free_term[0], c * ROWS, ROWS, 0)
    groups = range(GROUPS)

    start = jnp.concatenate([lax.dynamic_slice_in_dim(own, c * BLOCK, BLOCK, 0), f], 0)
    start = lax.ppermute(start, "tm", [(4 * k + 3, 4 * k + 2) for k in groups])
    down = [(2 * j + 1, 2 * j) for j in range(PARTS // 2)]
    other = lax.ppermute(own, "tm", down)
    f_odd = lax.ppermute(f, "tm", down)
    even_mats = halves(own)
    odd_mats = halves(other)
    inner = [(4 * k + 2, 4 * k) for k in groups]

    rows = tall(start, f, *even_mats)
    rows = lax.ppermute(rows, "tm", inner)
    rows = tall(rows, f_odd, *odd_mats)
    rows = tall(rows, f, *even_mats)
    term = rows[BLOCK:]
    rows = rows[:BLOCK]
    blocks = [rows] + around(rows, [4 * k for k in groups])
    group_mats = call(place_body, [shape(N, N, dtype=BF16)] * 2, [SMEM] + [VMEM] * 4, (meta, *blocks))

    zero = jnp.zeros((ROWS, N), F32)
    mats = (*odd_mats, *even_mats)
    terms = (f_odd, f)
    states = (zero, zero, zero)
    chips = TOP // 2
    half = chips // 2
    got = zero
    for i in range(chips):
        device = PARTS - 2 - 2 * i
        if i:
            pairs = [(device + 2, device)]
            mate = i + half if i + half < chips else i - half
            if 0 < mate < chips:
                at = PARTS - 2 - 2 * mate
                pairs.append((at + 2, at))
            got = lax.ppermute(states[2], "tm", sorted(pairs))
        states = two_steps(lambda at, device=device: at == device, meta, got, states, terms, mats)
    x_in, x_odd, x_even = states
    for k in reversed(groups):
        got = lax.ppermute(x_even, "tm", [(4 * k + 4, 4 * k)])
        x_in, x_even = one_step(lambda at, k=k: at == 4 * k, meta, got, (x_in, x_even), term, group_mats)
    got = lax.ppermute(x_even, "tm", [(4 * k + 4, 4 * k + 2) for k in groups])
    states = two_steps(lambda at: (at % 4 == 2) & (at < 4 * GROUPS), meta, got, (x_in, x_odd, x_even), terms, mats)
    x_in, x_odd, x_even = states
    got = lax.ppermute(x_even, "tm", inner)
    x_in, x_odd = one_step(lambda at: (at % 4 == 0) & (at < 4 * GROUPS), meta, got, (x_in, x_odd), f_odd, odd_mats)

    up = [(b, a) for a, b in down]
    pair = lax.ppermute(jnp.concatenate([x_odd, x_in], 0), "tm", up)
    pair = jnp.where(me % 2 == 1, pair, jnp.concatenate([x_even, x_odd], 0))
    blocks = [pair] + around(pair, range(PARTS))
    left = halves(slab_left[0].reshape(4 * N, BLOCK))
    right = halves(slab_right[0].reshape(4 * N, BLOCK))
    x, slab = call(
        slab_body,
        [shape(64, N), shape(4, 64, BLOCK)],
        [SMEM] + [VMEM] * 8,
        (meta, *blocks, *left, *right),
        12 * 64 * N * N,
        scratch_shapes=[pltpu.VMEM((64, N), F32)],
    )
    columns = lax.dynamic_slice_in_dim(x, c * BLOCK, BLOCK, 1)
    total = jnp.dot(arrow_rows[0], columns.T, precision=lax.Precision.HIGHEST, preferred_element_type=F32)
    behind, ahead, across = around(total, range(PARTS))
    total = (total + across) + (behind + ahead)
    for bit in (1, 2, 4, 8, 16, 32):
        total = total + lax.ppermute(total, "tm", [(j, j ^ bit) for j in range(PARTS)])
    return (columns[None], slab[None], corner_base + total)


def solution(mesh):
    placed = (
        P("tm", None, None),
        P("tm", None, None),
        P("tm", None, None, "col"),
        P("tm", None, None, "col"),
        P("tm", None, "col"),
        P(),
    )
    return jax.shard_map(
        local,
        mesh=mesh,
        in_specs=placed,
        out_specs=(P("tm", None, "col"), P("tm", None, None, "col"), P()),
        check_vma=False,
    )
```

time: 793 us -> 234 us (0.30)
  waiting for transfers between devices: 540 us -> 140 us
  blocking collectives: 108 us -> 0 us
  starting transfers between devices: 126 us -> 42 us
  Pallas kernels: 0 us -> 30.1 us
  matrix products: 13.4 us -> 0.2 us
  local copies, waits for them, and re-layouts: 2.41 us -> 15.5 us
    ppermute x64 -> x42, waiting for transfers between devices: 540 us -> 140 us  [the longest x1 116 us: local(): pair = lax.ppermute(jnp.concatenate([x_odd, x_in], 0), 'tm', up)]
    psum x1 -> x0, blocking collectives: 108 us -> none  [local(): corner = corner_base + lax.psum(partial_value, ('tm', 'col'))]
    ppermute x64 -> x42, starting transfers between devices: 126 us -> 42 us  [the longest x9 12.2 us: around(): lax.ppermute(value, ('tm', 'col'), [(t * COLS + j, t * COLS + (j + by) %...]
    pallas_call x0 -> x32, Pallas kernels: none -> 30.1 us  [the longest x28 24.7 us: call(): pl.pallas_call(body, out_shape=outs, in_specs=specs, out_specs=[VMEM] * l...]
    dot_general x4 -> x1, matrix products: 13.4 us -> 0.2 us  [local(): jnp.dot(arrow_rows[0], columns.T, precision=lax.Precision.HIGHEST, prefer...]
    unnamed x9 -> x34, local copies, waits for them, and re-layouts: 1.77 us -> 11.3 us
  transfers between devices with their start and end apart: 64 -> 42, of which waited for: 63 -> 10; matrix products, arithmetic and copies ran while one was open for 1% -> 1% of each run, Pallas kernels for 0% -> 7%
where the time goes in v1:
time: 234 us; the launch traced here: 230 us
  waiting for transfers between devices  140 us (60%)
  starting transfers between devices  42 us (18%)
  Pallas kernels  30.1 us (13%)
  local copies, waits for them, and re-layouts  15.5 us (7%)
    ppermute x1, waiting for transfers between devices, local(): pair = lax.ppermute(jnp.concatenate([x_odd, x_in], 0), 'tm', up)  116 us
    pallas_call x28, Pallas kernels, call(): pl.pallas_call(body, out_shape=outs, in_specs=specs, out_specs=[VMEM] * l...  24.7 us
    ppermute x6, waiting for transfers between devices, local(): lax.ppermute(total, 'tm', [(j, j ^ bit) for j in range(PARTS)])  19.5 us
    ppermute x9, starting transfers between devices, around(): lax.ppermute(value, ('tm', 'col'), [(t * COLS + j, t * COLS + (j + by) %...  12.2 us
    unnamed x34, local copies, waits for them, and re-layouts  11.3 us
    ppermute x11, starting transfers between devices, local(): got = lax.ppermute(x_even, 'tm', [(4 * k + 4, 4 * k)])  7.44 us
    ppermute x1, starting transfers between devices, local(): other = lax.ppermute(own, 'tm', down)  7.3 us
    ppermute x9, starting transfers between devices, local(): got = lax.ppermute(states[2], 'tm', sorted(pairs))  5.98 us
  transfers between devices with their start and end apart: 42, of which 10 were waited for; matrix products, arithmetic and copies ran while one was open for 1% of the time, Pallas kernels for 7%

profile of v1, /device:TPU:1, one launch (start us, length us, event | category | flops | bytes accessed | tf_op | source)
XLA Modules:
  0.0 229.8 jit_solution(4517578796409071567)
XLA Ops:
  0.6 7.3 %collective-permute-start.1 = (f32[1024,1024]{1,0:T(8,128)}, f32[1024,1024]{1,0:T(8,128)}, u32[]{:S(2)}, u32[]{:S(2)}) collective-permute-start(f32[1024,1024]{1,0:T(8,128)} %bitcast.20), channel_id=1, source_target_pairs={{4,0},{12,8},{20,16},{28,24},{36,32},{44,40},{52,48},{60,56},{68,6... | collective-permute-start | bytes 12582920 | tf_op jit(solution)/shard_map/ppermute | solution.py:168
  8.0 1.5 dynamic-slice_bitcast_fusion
  11.1 1.9 shard_map.97
  13.8 1.3 collective-permute-start
  15.1 3.1 %shard_map.85 = (bf16[1024,1024]{1,0:T(8,128)(2,1)S(1)}, bf16[1024,1024]{1,0:T(8,128)(2,1)S(1)}) custom-call(f32[1024,1024]{1,0:T(8,128)} %collective-permute-done.1.value_ref), custom_call_target="tpu_custom_call" | custom-call | flops 2097152 | bytes 8388608 | tf_op jit(solution)/shard_map/pallas_call | solution.py:142
  18.3 1.9 shard_map.98.left_ref
  20.3 1.9 shard_map.99
  23.3 1.2 slice.9.b0
  24.4 1.7 collective-permute-start.14
  26.1 1.6 collective-permute-start.15
  27.7 1.7 collective-permute-start.16
  29.5 1.6 copy-done.2
  31.1 1.6 copy-done.5
  32.7 1.6 copy-done.8
  48.0 2.8 %shard_map.100 = (bf16[1024,1024]{1,0:T(8,128)(2,1)S(1)}, bf16[1024,1024]{1,0:T(8,128)(2,1)S(1)}) custom-call(s32[5]{0:T(128)S(1)} %stack.23.meta.place_ref, f32[256,1024]{1,0:T(8,128)} %slice.9.b0, f32[256,1024]{1,0:T(8,128)} %collective-permute-done.14.b1, f32[256,1024]{1,0:T(8,128)} %collective-permute-done.15.b2, f32[256,1024]{1,0:T(8,128)} %collective-permute-done.16.b3), custom_call_target="tpu_custom_call" | custom-call | bytes 4194304 | tf_op jit(solution)/shard_map/pallas_call | solution.py:35
  67.9 1.3 collective-permute-start.29
  69.2 115.8 %collective-permute-done.29 = f32[32,1024]{1,0:T(8,128)S(1)} collective-permute-done((f32[32,1024]{1,0:T(8,128)S(1)}, f32[32,1024]{1,0:T(8,128)S(1)}, u32[]{:S(2)}, u32[]{:S(2)}) %collective-permute-start.29) | collective-permute-done | bytes 131104 | tf_op jit(solution)/shard_map/ppermute | solution.py:211
  185.0 1.4 collective-permute-start.30
  186.3 1.5 collective-permute-start.31
  187.9 1.6 collective-permute-start.32
  189.4 2.2 copy-done.12
  192.5 1.4 copy-done.13
  195.3 2.7 %shard_map.116 = (f32[64,1024]{1,0:T(8,128)S(1)}, f32[4,64,256]{2,1,0:T(8,128)}) custom-call(s32[5]{0:T(128)S(1)} %stack.23.meta.place_ref, f32[32,1024]{1,0:T(8,128)S(1)} %maximum_select_fusion.b0, f32[32,1024]{1,0:T(8,128)S(1)} %collective-permute-done.30.b1, f32[32,1024]{1,0:T(8,128)S(1)} %collective-permute-done.31.b2, ...), custom_call_target="tpu_custom_call" | custom-call | flops 805306368 | bytes 4194304 | tf_op jit(solution)/shard_map/pallas_call | solution.py:35
  198.8 2.1 collective-permute-start.35
  200.9 1.3 collective-permute-done.34
  202.2 3.0 %collective-permute-done.33 = f32[64,64]{0,1:T(8,128)S(1)} collective-permute-done((f32[64,64]{0,1:T(8,128)S(1)}, f32[64,64]{0,1:T(8,128)S(1)}, u32[]{:S(2)}, u32[]{:S(2)}) %collective-permute-start.33) | collective-permute-done | bytes 16416 | tf_op jit(solution)/shard_map/ppermute | solution.py:154
  205.2 2.8 %collective-permute-start.36 = (f32[64,64]{0,1:T(8,128)S(1)}, f32[64,64]{0,1:T(8,128)S(1)}, u32[]{:S(2)}, u32[]{:S(2)}) collective-permute-start(f32[64,64]{0,1:T(8,128)S(1)} %add_add_fusion.1), channel_id=1, source_target_pairs={{0,4},{4,0},{8,12},{12,8},{16,20},{20,16},{24,28},{28,24},{32,36},... | collective-permute-start | bytes 49160 | tf_op jit(solution)/shard_map/ppermute | solution.py:229
  208.8 2.8 %collective-permute-done.37 = f32[64,64]{0,1:T(8,128)S(1)} collective-permute-done((f32[64,64]{0,1:T(8,128)S(1)}, f32[64,64]{0,1:T(8,128)S(1)}, u32[]{:S(2)}, u32[]{:S(2)}) %collective-permute-start.37) | collective-permute-done | bytes 16416 | tf_op jit(solution)/shard_map/ppermute | solution.py:229
  212.4 3.5 %collective-permute-done.38 = f32[64,64]{0,1:T(8,128)S(1)} collective-permute-done((f32[64,64]{0,1:T(8,128)S(1)}, f32[64,64]{0,1:T(8,128)S(1)}, u32[]{:S(2)}, u32[]{:S(2)}) %collective-permute-start.38) | collective-permute-done | bytes 16416 | tf_op jit(solution)/shard_map/ppermute | solution.py:229
  215.9 2.8 %collective-permute-done.39 = f32[64,64]{0,1:T(8,128)S(1)} collective-permute-done((f32[64,64]{0,1:T(8,128)S(1)}, f32[64,64]{0,1:T(8,128)S(1)}, u32[]{:S(2)}, u32[]{:S(2)}) %collective-permute-start.39) | collective-permute-done | bytes 16416 | tf_op jit(solution)/shard_map/ppermute | solution.py:229
  218.8 3.6 %collective-permute-done.40 = f32[64,64]{0,1:T(8,128)S(1)} collective-permute-done((f32[64,64]{0,1:T(8,128)S(1)}, f32[64,64]{0,1:T(8,128)S(1)}, u32[]{:S(2)}, u32[]{:S(2)}) %collective-permute-start.40) | collective-permute-done | bytes 16416 | tf_op jit(solution)/shard_map/ppermute | solution.py:229
  223.1 6.0 %collective-permute-done.41 = f32[64,64]{0,1:T(8,128)S(1)} collective-permute-done((f32[64,64]{0,1:T(8,128)S(1)}, f32[64,64]{0,1:T(8,128)S(1)}, u32[]{:S(2)}, u32[]{:S(2)}) %collective-permute-start.41) | collective-permute-done | bytes 16416 | tf_op jit(solution)/shard_map/ppermute | solution.py:229
  (139 shorter events, 40.1 us)
Async XLA Ops:
  0.6 14.4 %collective-permute-start.1 = (f32[1024,1024]{1,0:T(8,128)}, f32[1024,1024]{1,0:T(8,128)}, u32[]{:S(2)}, u32[]{:S(2)}) collective-permute-start(f32[1024,1024]{1,0:T(8,128)} %bitcast.20), channel_id=1, source_target_pairs={{4,0},{12,8},{20,16},{28,24},{36,32},{44,40},{52,48},{60,56},{68,6... | collective-permute-start | bytes 12582920 | tf_op jit(solution)/shard_map/ppermute | solution.py:168
  9.6 1.6 collective-permute-start.12
  13.0 5.2 %collective-permute-start.13 = (f32[272,1024]{1,0:T(8,128)S(1)}, f32[272,1024]{1,0:T(8,128)S(1)}, u32[]{:S(2)}, u32[]{:S(2)}) collective-permute-start(f32[272,1024]{1,0:T(8,128)S(1)} %shard_map.97), channel_id=1, source_target_pairs={{8,0},{24,16},{40,32},{56,48},{72,64},{88,80},{104,96},{120,112},{... | collective-permute-start | bytes 3342344 | tf_op jit(solution)/shard_map/ppermute | solution.py:175
  13.8 4.5 %collective-permute-start = (f32[16,1024]{1,0:T(8,128)S(1)}, f32[16,1024]{1,0:T(8,128)S(1)}, u32[]{:S(2)}, u32[]{:S(2)}) collective-permute-start(f32[16,1024]{1,0:T(8,128)S(1)} %dynamic-slice_bitcast_fusion.1.fe.bias_ref), channel_id=1, source_target_pairs={{4,0},{12,8},{20,16},{28,24},{36,32},{44,40},{52,48},{60,56},{68,6... | collective-permute-start | bytes 196616 | tf_op jit(solution)/shard_map/ppermute | solution.py:169
  24.4 23.5 %collective-permute-start.14 = (f32[256,1024]{1,0:T(8,128)}, f32[256,1024]{1,0:T(8,128)}, u32[]{:S(2)}, u32[]{:S(2)}) collective-permute-start(f32[256,1024]{1,0:T(8,128)} %slice.9.b0), channel_id=1, source_target_pairs={{0,1},{1,2},{2,3},{3,0},{16,17},{17,18},{18,19},{19,16},{32,33},{3... | collective-permute-start | bytes 3145736 | tf_op jit(solution)/shard_map/ppermute | solution.py:154
  26.1 21.9 %collective-permute-start.15 = (f32[256,1024]{1,0:T(8,128)}, f32[256,1024]{1,0:T(8,128)}, u32[]{:S(2)}, u32[]{:S(2)}) collective-permute-start(f32[256,1024]{1,0:T(8,128)} %slice.9.b0), channel_id=1, source_target_pairs={{0,3},{1,0},{2,1},{3,2},{16,19},{17,16},{18,17},{19,18},{32,35},{3... | collective-permute-start | bytes 3145736 | tf_op jit(solution)/shard_map/ppermute | solution.py:154
  27.7 20.2 %collective-permute-start.16 = (f32[256,1024]{1,0:T(8,128)}, f32[256,1024]{1,0:T(8,128)}, u32[]{:S(2)}, u32[]{:S(2)}) collective-permute-start(f32[256,1024]{1,0:T(8,128)} %slice.9.b0), channel_id=1, source_target_pairs={{0,2},{1,3},{2,0},{3,1},{16,18},{17,19},{18,16},{19,17},{32,34},{3... | collective-permute-start | bytes 3145736 | tf_op jit(solution)/shard_map/ppermute | solution.py:154
  34.9 0.7 collective-permute-start.2
  36.1 0.7 collective-permute-start.3
  37.4 0.7 collective-permute-start.4
  38.7 0.7 collective-permute-start.5
  39.9 0.7 collective-permute-start.6
  41.2 0.7 collective-permute-start.7
  42.7 0.7 collective-permute-start.8
  43.9 0.7 collective-permute-start.9
  46.5 4.3 %collective-permute-start.11 = (f32[16,1024]{1,0:T(8,128)S(1)}, f32[16,1024]{1,0:T(8,128)S(1)}, u32[]{:S(2)}, u32[]{:S(2)}) collective-permute-start(f32[16,1024]{1,0:T(8,128)S(1)} %get-tuple-element.103.state_0), channel_id=1, source_target_pairs={{176,160},{177,161},{178,162},{179,163}} | collective-permute-start | bytes 196616 | tf_op jit(solution)/shard_map/ppermute | solution.py:202
  62.7 0.8 collective-permute-start.26
  64.1 0.8 collective-permute-start.27
  66.4 0.7 collective-permute-start.28
  67.9 117.1 %collective-permute-start.29 = (f32[32,1024]{1,0:T(8,128)S(1)}, f32[32,1024]{1,0:T(8,128)S(1)}, u32[]{:S(2)}, u32[]{:S(2)}) collective-permute-start(f32[32,1024]{1,0:T(8,128)S(1)} %pad_maximum_fusion.1), channel_id=1, source_target_pairs={{0,4},{8,12},{16,20},{24,28},{32,36},{40,44},{48,52},{56,60},{64,6... | collective-permute-start | bytes 393224 | tf_op jit(solution)/shard_map/ppermute | solution.py:211
  185.0 9.7 %collective-permute-start.30 = (f32[32,1024]{1,0:T(8,128)S(1)}, f32[32,1024]{1,0:T(8,128)S(1)}, u32[]{:S(2)}, u32[]{:S(2)}) collective-permute-start(f32[32,1024]{1,0:T(8,128)S(1)} %maximum_select_fusion.b0), channel_id=1, source_target_pairs={{0,1},{1,2},{2,3},{3,0},{4,5},{5,6},{6,7},{7,4},{8,9},{9,10},{10,1... | collective-permute-start | bytes 393224 | tf_op jit(solution)/shard_map/ppermute | solution.py:154
  186.3 8.3 %collective-permute-start.31 = (f32[32,1024]{1,0:T(8,128)S(1)}, f32[32,1024]{1,0:T(8,128)S(1)}, u32[]{:S(2)}, u32[]{:S(2)}) collective-permute-start(f32[32,1024]{1,0:T(8,128)S(1)} %maximum_select_fusion.b0), channel_id=1, source_target_pairs={{0,3},{1,0},{2,1},{3,2},{4,7},{5,4},{6,5},{7,6},{8,11},{9,8},{10,9... | collective-permute-start | bytes 393224 | tf_op jit(solution)/shard_map/ppermute | solution.py:154
  187.9 7.4 %collective-permute-start.32 = (f32[32,1024]{1,0:T(8,128)S(1)}, f32[32,1024]{1,0:T(8,128)S(1)}, u32[]{:S(2)}, u32[]{:S(2)}) collective-permute-start(f32[32,1024]{1,0:T(8,128)S(1)} %maximum_select_fusion.b0), channel_id=1, source_target_pairs={{0,2},{1,3},{2,0},{3,1},{4,6},{5,7},{6,4},{7,5},{8,10},{9,11},{10,... | collective-permute-start | bytes 393224 | tf_op jit(solution)/shard_map/ppermute | solution.py:154
  198.2 4.1 %collective-permute-start.34 = (f32[64,64]{0,1:T(8,128)S(1)}, f32[64,64]{0,1:T(8,128)S(1)}, u32[]{:S(2)}, u32[]{:S(2)}) collective-permute-start(f32[64,64]{0,1:T(8,128)S(1)} %convolution_bitcast_fusion), channel_id=1, source_target_pairs={{0,1},{1,2},{2,3},{3,0},{4,5},{5,6},{6,7},{7,4},{8,9},{9,10},{10,1... | collective-permute-start | bytes 49160 | tf_op jit(solution)/shard_map/ppermute | solution.py:154
  198.8 3.4 %collective-permute-start.35 = (f32[64,64]{0,1:T(8,128)S(1)}, f32[64,64]{0,1:T(8,128)S(1)}, u32[]{:S(2)}, u32[]{:S(2)}) collective-permute-start(f32[64,64]{0,1:T(8,128)S(1)} %convolution_bitcast_fusion), channel_id=1, source_target_pairs={{0,3},{1,0},{2,1},{3,2},{4,7},{5,4},{6,5},{7,6},{8,11},{9,8},{10,9... | collective-permute-start | bytes 49160 | tf_op jit(solution)/shard_map/ppermute | solution.py:154
  200.9 4.3 %collective-permute-start.33 = (f32[64,64]{0,1:T(8,128)S(1)}, f32[64,64]{0,1:T(8,128)S(1)}, u32[]{:S(2)}, u32[]{:S(2)}) collective-permute-start(f32[64,64]{0,1:T(8,128)S(1)} %convolution_bitcast_fusion), channel_id=1, source_target_pairs={{0,2},{1,3},{2,0},{3,1},{4,6},{5,7},{6,4},{7,5},{8,10},{9,11},{10,... | collective-permute-start | bytes 49160 | tf_op jit(solution)/shard_map/ppermute | solution.py:154
  205.2 3.6 %collective-permute-start.36 = (f32[64,64]{0,1:T(8,128)S(1)}, f32[64,64]{0,1:T(8,128)S(1)}, u32[]{:S(2)}, u32[]{:S(2)}) collective-permute-start(f32[64,64]{0,1:T(8,128)S(1)} %add_add_fusion.1), channel_id=1, source_target_pairs={{0,4},{4,0},{8,12},{12,8},{16,20},{20,16},{24,28},{28,24},{32,36},... | collective-permute-start | bytes 49160 | tf_op jit(solution)/shard_map/ppermute | solution.py:229
  208.8 2.8 %collective-permute-start.37 = (f32[64,64]{0,1:T(8,128)S(1)}, f32[64,64]{0,1:T(8,128)S(1)}, u32[]{:S(2)}, u32[]{:S(2)}) collective-permute-start(f32[64,64]{0,1:T(8,128)S(1)} %add.71), channel_id=1, source_target_pairs={{0,8},{4,12},{8,0},{12,4},{16,24},{20,28},{24,16},{28,20},{32,40},... | collective-permute-start | bytes 49160 | tf_op jit(solution)/shard_map/ppermute | solution.py:229
  211.6 4.3 %collective-permute-start.38 = (f32[64,64]{0,1:T(8,128)S(1)}, f32[64,64]{0,1:T(8,128)S(1)}, u32[]{:S(2)}, u32[]{:S(2)}) collective-permute-start(f32[64,64]{0,1:T(8,128)S(1)} %add.72), channel_id=1, source_target_pairs={{0,16},{4,20},{8,24},{12,28},{16,0},{20,4},{24,8},{28,12},{32,48},... | collective-permute-start | bytes 49160 | tf_op jit(solution)/shard_map/ppermute | solution.py:229
  215.9 2.8 %collective-permute-start.39 = (f32[64,64]{0,1:T(8,128)S(1)}, f32[64,64]{0,1:T(8,128)S(1)}, u32[]{:S(2)}, u32[]{:S(2)}) collective-permute-start(f32[64,64]{0,1:T(8,128)S(1)} %add.73), channel_id=1, source_target_pairs={{0,32},{4,36},{8,40},{12,44},{16,48},{20,52},{24,56},{28,60},{32,0... | collective-permute-start | bytes 49160 | tf_op jit(solution)/shard_map/ppermute | solution.py:229
  218.7 3.7 %collective-permute-start.40 = (f32[64,64]{0,1:T(8,128)S(1)}, f32[64,64]{0,1:T(8,128)S(1)}, u32[]{:S(2)}, u32[]{:S(2)}) collective-permute-start(f32[64,64]{0,1:T(8,128)S(1)} %add.74), channel_id=1, source_target_pairs={{0,64},{4,68},{8,72},{12,76},{16,80},{20,84},{24,88},{28,92},{32,9... | collective-permute-start | bytes 49160 | tf_op jit(solution)/shard_map/ppermute | solution.py:229
  222.4 6.7 %collective-permute-start.41 = (f32[64,64]{0,1:T(8,128)S(1)}, f32[64,64]{0,1:T(8,128)S(1)}, u32[]{:S(2)}, u32[]{:S(2)}) collective-permute-start(f32[64,64]{0,1:T(8,128)S(1)} %add.75), channel_id=1, source_target_pairs={{0,128},{4,132},{8,136},{12,140},{16,144},{20,148},{24,152},{28,15... | collective-permute-start | bytes 49160 | tf_op jit(solution)/shard_map/ppermute | solution.py:229
  (26 other events, 72.7 us)

commit v2 on v1

v2 whole, which is shorter than its diff:
```python
import functools
import jax
import jax.numpy as jnp
from jax import lax
from jax.experimental import pallas as pl
from jax.experimental.pallas import tpu as pltpu
from jax.sharding import PartitionSpec as P

PARTS = 64
N = 1024
COLS = 4
ROWS = 16
BLOCK = 256
TOP = 24
GROUPS = (PARTS - TOP) // 4
F32 = jnp.float32
BF16 = jnp.bfloat16
VMEM = pl.BlockSpec(memory_space=pltpu.VMEM)


def split(value):
    high = value.astype(BF16)
    return high, (value - high.astype(F32)).astype(BF16)


def product(left, high, low):
    rows = left.shape[0]
    left_high, left_low = split(left)
    both = jnp.dot(jnp.concatenate([left_high, left_low], 0), high, preferred_element_type=F32)
    return both[:rows] + both[rows:] + jnp.dot(left_high, low, preferred_element_type=F32)


def call(body, outs, specs, operands, flops=0, limit=8, **kw):
    return pl.pallas_call(
        body,
        out_shape=outs,
        in_specs=specs,
        out_specs=[VMEM] * len(outs),
        compiler_params=pltpu.CompilerParams(vmem_limit_bytes=limit << 20),
        cost_estimate=pl.CostEstimate(flops=flops, bytes_accessed=4 << 20, transcendentals=0),
        **kw,
    )(*operands)


def shape(*dims, dtype=F32):
    return jax.ShapeDtypeStruct(dims, dtype)


def when_at(test, run):
    pl.when(test(lax.axis_index("tm")))(run)


def upper_chip(at):
    return (at % 4 == 2) & (at < 4 * GROUPS)


def lower_chip(at):
    return (at % 4 == 0) & (at < 4 * GROUPS)


def moved(at):
    return (at % 8 == 2) & (at < 4 * GROUPS)


def home(k):
    return 4 * k + 2 if k % 2 == 0 else 4 * k


def is_home(at):
    return ((at % 8 == 2) | (at % 8 == 4)) & (at < 4 * GROUPS)


def tall_body(test, left_ref, bias_ref, high_ref, low_ref, out_ref):
    def run():
        out_ref[...] = product(left_ref[...], high_ref[...], low_ref[...])
        out_ref[BLOCK:, :] += bias_ref[...]

    when_at(test, run)


def tall(test, left, bias, high, low):
    (out,) = call(
        functools.partial(tall_body, test),
        [shape(BLOCK + ROWS, N)],
        [VMEM] * 4,
        (left, bias, high, low),
        6 * 272 * N * N,
    )
    return out


def pick_body(own_ref, got_ref, rows_ref, term_ref):
    def take(source):
        rows_ref[...] = source[:BLOCK, :]
        term_ref[...] = source[BLOCK:, :]

    when_at(moved, lambda: take(got_ref))
    when_at(lambda at: jnp.logical_not(moved(at)), lambda: take(own_ref))


def two_body(tests, *refs):
    count = len(tests)
    gots, (in_0, odd_0, even_0, fo, fe, oh, ol, eh, el, in_1, odd_1, even_1) = refs[:count], refs[count:]

    def step(got):
        x = got[...]
        odd = product(x, oh[...], ol[...]) + fo[...]
        in_1[...] = x
        odd_1[...] = odd
        even_1[...] = product(odd, eh[...], el[...]) + fe[...]

    for test, got in zip(tests, gots):
        when_at(test, functools.partial(step, got))


def two_steps(tests, gots, states, terms, mats):
    count = len(gots)
    return call(
        functools.partial(two_body, tests),
        [shape(ROWS, N)] * 3,
        [VMEM] * (9 + count),
        (*gots, *states, *terms, *mats),
        12 * 16 * N * N,
        input_output_aliases={count: 0, count + 1: 1, count + 2: 2},
    )


def one_body(test, got, in_0, state_0, term, high, low, in_1, state_1):
    def run():
        x = got[...]
        in_1[...] = x
        state_1[...] = product(x, high[...], low[...]) + term[...]

    when_at(test, run)


def one_step(test, got, states, term, mats):
    return call(
        functools.partial(one_body, test),
        [shape(ROWS, N)] * 2,
        [VMEM] * 6,
        (got, *states, term, *mats),
        6 * 16 * N * N,
        input_output_aliases={1: 0, 2: 1},
    )


def places():
    c = lax.axis_index("col")
    return [c, (c + 3) % COLS, (c + 1) % COLS, (c + 2) % COLS]


def place_body(b0, b1, b2, b3, high_ref, low_ref):
    def run():
        for place, block in zip(places(), (b0, b1, b2, b3)):
            high, low = split(block[...])
            at = pl.ds(pl.multiple_of(place * BLOCK, BLOCK), BLOCK)
            high_ref[at, :] = high
            low_ref[at, :] = low

    when_at(is_home, run)


def slab_body(b0, b1, b2, b3, lh, ll, rh, rl, own_ref, out_ref, x_ref, next_ref):
    for place, block in zip(places(), (b0, b1, b2, b3)):
        at = pl.ds(pl.multiple_of(place * ROWS, ROWS), ROWS)
        x_ref[at, :] = block[:ROWS, :]
        next_ref[at, :] = block[ROWS:, :]
    own = x_ref[...]
    later = next_ref[...]
    own_ref[...] = x_ref[:, pl.ds(pl.multiple_of(places()[0] * BLOCK, BLOCK), BLOCK)]
    for k in range(4):
        at = slice(k * N, k * N + N)
        out_ref[k] = product(own, lh[at, :], ll[at, :]) + product(later, rh[at, :], rl[at, :])


def finish_body(in_ref, odd_ref, even_ref, arrow_odd, arrow_even, send_ref, keep_ref, total_ref):
    send_ref[:ROWS, :] = odd_ref[...]
    send_ref[ROWS:, :] = in_ref[...]
    keep_ref[:ROWS, :] = even_ref[...]
    keep_ref[ROWS:, :] = odd_ref[...]

    def across(x, arrow):
        (x_high, x_low), (high, low) = split(x), split(arrow)
        dims = (((1,), (1,)), ((), ()))
        both = lax.dot_general(jnp.concatenate([x_high, x_low], 0), high, dims, preferred_element_type=F32)
        return both[:ROWS] + both[ROWS:] + lax.dot_general(x_high, low, dims, preferred_element_type=F32)

    total_ref[...] = across(even_ref[...], arrow_even[...]) + across(odd_ref[...], arrow_odd[...])


def choose_body(got_ref, keep_ref, out_ref):
    def take(source):
        out_ref[...] = source[...]

    when_at(lambda at: at % 2 == 1, lambda: take(got_ref))
    when_at(lambda at: at % 2 == 0, lambda: take(keep_ref))


def choose(got, keep):
    (out,) = call(choose_body, [shape(*keep.shape)], [VMEM] * 2, (got, keep))
    return out


def arrow_body(b0, b1, b2, b3, out_ref):
    for place, block in zip(places(), (b0, b1, b2, b3)):
        out_ref[:, pl.ds(pl.multiple_of(place * BLOCK, BLOCK), BLOCK)] = block[...]


def corner_body(base_ref, b0, b1, b2, b3, out_ref, rows_ref):
    for place, block in zip(places(), (b0, b1, b2, b3)):
        rows_ref[pl.ds(pl.multiple_of(place * ROWS, ROWS), ROWS), :] = block[...]
    out_ref[...] = base_ref[...] + rows_ref[...].T


def split_body(value_ref, high_ref, low_ref):
    high_ref[...], low_ref[...] = split(value_ref[...])


def halves(value):
    rows, columns = value.shape
    tile = pl.BlockSpec((BLOCK, columns), lambda i: (i, 0))
    return pl.pallas_call(
        split_body,
        grid=(rows // BLOCK,),
        out_shape=[shape(rows, columns, dtype=BF16)] * 2,
        in_specs=[tile],
        out_specs=[tile, tile],
        compiler_params=pltpu.CompilerParams(vmem_limit_bytes=8 << 20),
        cost_estimate=pl.CostEstimate(flops=2 * rows * columns, bytes_accessed=8 * rows * columns, transcendentals=0),
    )(value)


def around(value, members):
    return [lax.ppermute(value, ("tm", "col"), [(t * COLS + j, t * COLS + (j + by) % COLS) for t in members for j in range(COLS)]) for by in (1, 3, 2)]


def local(couple, free_term, slab_left, slab_right, arrow_rows, corner_base):
    c = lax.axis_index("col")
    own = couple[0]
    f = lax.dynamic_slice_in_dim(free_term[0], c * ROWS, ROWS, 0)
    groups = range(GROUPS)
    down = [(2 * j + 1, 2 * j) for j in range(PARTS // 2)]
    up = [(b, a) for a, b in down]
    inner = [(4 * k + 2, 4 * k) for k in groups]

    start = jnp.concatenate([lax.dynamic_slice_in_dim(own, c * BLOCK, BLOCK, 0), f], 0)
    start = lax.ppermute(start, "tm", [(4 * k + 3, 4 * k + 2) for k in groups])
    other = lax.ppermute(own, "tm", down)
    f_odd = lax.ppermute(f, "tm", down)
    even_mats = halves(own)
    odd_mats = halves(other)
    mats = (*odd_mats, *even_mats)
    terms = (f_odd, f)
    rows = tall(upper_chip, start, f, *even_mats)
    zero = jnp.zeros((ROWS, N), F32)
    rows, zero = lax.optimization_barrier((rows, zero))
    rows = lax.ppermute(rows, "tm", inner)

    states = (zero, zero, zero)
    chips = TOP // 2
    half = chips // 2
    got = zero
    for i in range(chips):
        device = PARTS - 2 - 2 * i
        if i:
            pairs = [(device + 2, device)]
            mate = i + half if i + half < chips else i - half
            if 0 < mate < chips:
                at = PARTS - 2 - 2 * mate
                pairs.append((at + 2, at))
            got = lax.ppermute(states[2], "tm", sorted(pairs))
        states = two_steps([lambda at, device=device: at == device], [got], states, terms, mats)
    rows, states = lax.optimization_barrier((rows, states))

    rows = tall(lower_chip, rows, f_odd, *odd_mats)
    rows = tall(lower_chip, rows, f, *even_mats)
    moved_rows = lax.ppermute(rows, "tm", [(4 * k, 4 * k + 2) for k in groups if k % 2 == 0 and k > 0])
    rows, term = call(pick_body, [shape(BLOCK, N), shape(ROWS, N)], [VMEM] * 2, (rows, moved_rows))
    others = around(rows, [home(k) for k in groups if k > 0])

    rows, slab_left, slab_right, arrow_rows = lax.optimization_barrier((rows, slab_left, slab_right, arrow_rows))
    left = halves(slab_left[0].reshape(4 * N, BLOCK))
    right = halves(slab_right[0].reshape(4 * N, BLOCK))
    arrows = [arrow_rows[0]] + around(arrow_rows[0], range(PARTS))
    (arrow,) = call(arrow_body, [shape(64, N)], [VMEM] * 4, arrows)
    arrow_odd = lax.ppermute(arrow, "tm", down)
    others, left, right, arrow, arrow_odd, states = lax.optimization_barrier((others, left, right, arrow, arrow_odd, states))
    group_mats = call(place_body, [shape(N, N, dtype=BF16)] * 2, [VMEM] * 4, (rows, *others))

    x_in, x_odd, x_even = states
    message = x_even
    for k in reversed(groups):
        source = home(k + 1) if k + 1 < GROUPS else 4 * GROUPS
        pairs = [(source, home(k))]
        mate = (k + GROUPS // 2) % GROUPS
        pairs.append((home(mate + 1) if mate + 1 < GROUPS else 4 * GROUPS, home(mate)))
        got = lax.ppermute(message, "tm", sorted(pairs))
        if k:
            x_in, message = one_step(lambda at, k=k: at == home(k), got, (x_in, message), term, group_mats)
    last = got

    got = lax.ppermute(x_in, "tm", [(4 * k, 4 * k + 2) for k in groups if k % 2 == 1])
    x_in, x_odd, x_even = two_steps(
        [
            lambda at: at == home(0),
            lambda at: (at % 8 == 6) & (at < 4 * GROUPS),
            lambda at: moved(at) & (at != home(0)),
        ],
        [last, got, x_in],
        (x_in, x_odd, x_even),
        terms,
        mats,
    )
    got = lax.ppermute(x_even, "tm", inner)
    x_in, x_odd, x_even = two_steps([lower_chip], [got], (x_in, x_odd, x_even), terms, mats)

    send, keep, total = call(
        finish_body,
        [shape(2 * ROWS, N)] * 2 + [shape(ROWS, 64)],
        [VMEM] * 5,
        (x_in, x_odd, x_even, arrow_odd, arrow),
        12 * 16 * N * 64,
    )

    def exchange(total, bit):
        return total + lax.ppermute(total, "tm", [(j, j ^ bit) for j in range(0, PARTS, 2)])

    pair = lax.ppermute(send, "tm", up)
    total = exchange(total, 2)
    total, pair = lax.optimization_barrier((total, pair))
    pair = choose(pair, keep)
    blocks = around(pair, range(PARTS))
    total = exchange(total, 4)
    total, *blocks = lax.optimization_barrier((total, *blocks))
    columns, slab = call(
        slab_body,
        [shape(64, BLOCK), shape(4, 64, BLOCK)],
        [VMEM] * 8,
        (pair, *blocks, *left, *right),
        12 * 64 * N * N,
        scratch_shapes=[pltpu.VMEM((64, N), F32)] * 2,
    )
    for bit in (8, 16, 32):
        total = exchange(total, bit)
    total = choose(lax.ppermute(total, "tm", up), total)
    totals = [total] + around(total, range(PARTS))
    (corner,) = call(corner_body, [shape(64, 64)], [VMEM] * 5, (corner_base, *totals), scratch_shapes=[pltpu.VMEM((64, 64), F32)])
    return (columns[None], slab[None], corner)


def solution(mesh):
    placed = (
        P("tm", None, None),
        P("tm", None, None),
        P("tm", None, None, "col"),
        P("tm", None, None, "col"),
        P("tm", None, "col"),
        P(),
    )
    return jax.shard_map(
        local,
        mesh=mesh,
        in_specs=placed,
        out_specs=(P("tm", None, "col"), P("tm", None, None, "col"), P()),
        check_vma=False,
    )
```

time: 234 us -> 220 us (0.940); the launches traced: 230 us -> 219 us
  Pallas kernels: 30.1 us -> 9.64 us
  starting transfers between devices: 42 us -> 59.1 us
  local copies, waits for them, and re-layouts: 15.5 us -> 3.02 us
  waiting for transfers between devices: 140 us -> 145 us
    pallas_call x28 -> x34, Pallas kernels: 24.7 us -> 4.21 us  [call(): pl.pallas_call(body, out_shape=outs, in_specs=specs, out_specs=[VMEM] * l...]
    ppermute x19 -> x20, starting transfers between devices: 13.1 us -> 28.5 us  [the longest x1 14.5 us: local(): arrow_odd = lax.ppermute(arrow, 'tm', down)]
    unnamed x34 -> x17, local copies, waits for them, and re-layouts: 11.3 us -> 1.53 us
    ppermute x9 -> x12, waiting for transfers between devices: 4.87 us -> 10.7 us  [around(): lax.ppermute(value, ('tm', 'col'), [(t * COLS + j, t * COLS + (j + by) %...]
    ppermute x9 -> x11, starting transfers between devices: 5.98 us -> 7.31 us  [local(): got = lax.ppermute(states[2], 'tm', sorted(pairs))]
    ppermute x19 -> x20, waiting for transfers between devices: 135 us -> 134 us  [the longest x1 107 us: local(): pair = lax.ppermute(send, 'tm', up)]
    ppermute x9 -> x12, starting transfers between devices: 12.2 us -> 12.5 us  [around(): lax.ppermute(value, ('tm', 'col'), [(t * COLS + j, t * COLS + (j + by) %...]
  transfers between devices with their start and end apart: 42 -> 48, of which waited for: 10 -> 8; matrix products, arithmetic and copies ran while one was open for 1% -> 1% of each run, Pallas kernels for 7% -> 4%
where the time goes in v2:
time: 220 us; the launch traced here: 219 us
  waiting for transfers between devices  145 us (66%)
  starting transfers between devices  59.1 us (27%)
  Pallas kernels  9.64 us (4%)
  local copies, waits for them, and re-layouts  3.02 us (1%)
    ppermute x1, waiting for transfers between devices, local(): pair = lax.ppermute(send, 'tm', up)  107 us
    ppermute x1, waiting for transfers between devices, local(): total = choose(lax.ppermute(total, 'tm', up), total)  27.8 us
    ppermute x1, starting transfers between devices, local(): arrow_odd = lax.ppermute(arrow, 'tm', down)  14.5 us
    ppermute x12, starting transfers between devices, around(): lax.ppermute(value, ('tm', 'col'), [(t * COLS + j, t * COLS + (j + by) %...  12.5 us
    ppermute x12, waiting for transfers between devices, around(): lax.ppermute(value, ('tm', 'col'), [(t * COLS + j, t * COLS + (j + by) %...  10.7 us
    ppermute x11, starting transfers between devices, local(): got = lax.ppermute(states[2], 'tm', sorted(pairs))  7.31 us
    ppermute x1, starting transfers between devices, local(): other = lax.ppermute(own, 'tm', down)  7.3 us
    ppermute x10, starting transfers between devices, local(): got = lax.ppermute(message, 'tm', sorted(pairs))  6.65 us
  transfers between devices with their start and end apart: 48, of which 8 were waited for; matrix products, arithmetic and copies ran while one was open for 1% of the time, Pallas kernels for 4%

profile of v2, /device:TPU:1, one launch (start us, length us, event | category | flops | bytes accessed | tf_op | source)
XLA Modules:
  0.0 218.7 jit_solution(17729392816734962171)
XLA Ops:
  0.6 7.3 %collective-permute-start.3 = (f32[1024,1024]{1,0:T(8,128)}, f32[1024,1024]{1,0:T(8,128)}, u32[]{:S(2)}, u32[]{:S(2)}) collective-permute-start(f32[1024,1024]{1,0:T(8,128)} %bitcast.10), channel_id=1, source_target_pairs={{4,0},{12,8},{20,16},{28,24},{36,32},{44,40},{52,48},{60,56},{68,6... | collective-permute-start | bytes 12582920 | tf_op jit(solution)/shard_map/ppermute | solution.py:249
  8.0 1.5 dynamic-slice_bitcast_fusion
  9.6 0.7 collective-permute-start
  11.1 0.7 collective-permute-start.1
  11.8 1.3 collective-permute-start.2
  13.2 3.1 %shard_map.87 = (bf16[1024,1024]{1,0:T(8,128)(2,1)S(1)}, bf16[1024,1024]{1,0:T(8,128)(2,1)S(1)}) custom-call(f32[1024,1024]{1,0:T(8,128)} %collective-permute-done.3.value_ref), custom_call_target="tpu_custom_call" | custom-call | flops 2097152 | bytes 8388608 | tf_op jit(solution)/shard_map/pallas_call | solution.py:223
  16.4 0.7 collective-permute-start.4
  17.1 0.7 collective-permute-start.5
  17.8 0.7 collective-permute-start.6
  24.5 0.9 collective-permute-start.15
  25.5 0.9 collective-permute-start.16
  26.3 0.7 collective-permute-start.17
  27.1 0.7 collective-permute-start.18
  27.9 2.7 %collective-permute-start.20 = (f32[64,256]{1,0:T(8,128)S(1)}, f32[64,256]{1,0:T(8,128)S(1)}, u32[]{:S(2)}, u32[]{:S(2)}) collective-permute-start(f32[64,256]{1,0:T(8,128)S(1)} %bitcast.15), channel_id=1, source_target_pairs={{0,3},{1,0},{2,1},{3,2},{4,7},{5,4},{6,5},{7,6},{8,11},{9,8},{10,9... | collective-permute-start | bytes 196616 | tf_op jit(solution)/shard_map/ppermute | solution.py:235
  30.6 1.6 collective-permute-done.19.b1
  32.5 4.4 %collective-permute-done.21.b3 = f32[64,256]{1,0:T(8,128)S(1)} collective-permute-done((f32[64,256]{1,0:T(8,128)S(1)}, f32[64,256]{1,0:T(8,128)S(1)}, u32[]{:S(2)}, u32[]{:S(2)}) %collective-permute-start.21) | collective-permute-done | bytes 65568 | tf_op jit(solution)/shard_map/ppermute | solution.py:235
  36.9 14.5 %collective-permute-start.22 = (f32[64,1024]{1,0:T(8,128)S(1)}, f32[64,1024]{1,0:T(8,128)S(1)}, u32[]{:S(2)}, u32[]{:S(2)}) collective-permute-start(f32[64,1024]{1,0:T(8,128)S(1)} %shard_map.105.arrow_even), channel_id=1, source_target_pairs={{4,0},{12,8},{20,16},{28,24},{36,32},{44,40},{52,48},{60,56},{68,6... | collective-permute-start | bytes 786440 | tf_op jit(solution)/shard_map/ppermute | solution.py:287
  51.4 0.8 shard_map.103
  52.2 1.3 copy-done.3
  53.6 0.8 shard_map.104
  63.5 1.3 collective-permute-start.36
  65.5 106.5 %collective-permute-done.36.got_ref = f32[32,1024]{1,0:T(8,128)S(1)} collective-permute-done((f32[32,1024]{1,0:T(8,128)S(1)}, f32[32,1024]{1,0:T(8,128)S(1)}, u32[]{:S(2)}, u32[]{:S(2)}) %collective-permute-start.36) | collective-permute-done | bytes 131104 | tf_op jit(solution)/shard_map/ppermute | solution.py:329
  172.2 2.6 %collective-permute-start.39 = (f32[32,1024]{1,0:T(8,128)S(1)}, f32[32,1024]{1,0:T(8,128)S(1)}, u32[]{:S(2)}, u32[]{:S(2)}) collective-permute-start(f32[32,1024]{1,0:T(8,128)S(1)} %shard_map.119.b0), channel_id=1, source_target_pairs={{0,3},{1,0},{2,1},{3,2},{4,7},{5,4},{6,5},{7,6},{8,11},{9,8},{10,9... | collective-permute-start | bytes 393224 | tf_op jit(solution)/shard_map/ppermute | solution.py:235
  175.9 1.2 collective-permute-done.38.b1
  177.1 1.0 collective-permute-done.39.b2
  178.1 2.0 collective-permute-done.40.b3
  182.2 1.3 collective-permute-start.44
  183.5 27.8 %collective-permute-done.44.got_ref = f32[16,64]{1,0:T(8,128)S(1)} collective-permute-done((f32[16,64]{1,0:T(8,128)S(1)}, f32[16,64]{1,0:T(8,128)S(1)}, u32[]{:S(2)}, u32[]{:S(2)}) %collective-permute-start.44) | collective-permute-done | bytes 4128 | tf_op jit(solution)/shard_map/ppermute | solution.py:346
  211.7 2.3 %collective-permute-start.46 = (f32[16,64]{1,0:T(8,128)S(1)}, f32[16,64]{1,0:T(8,128)S(1)}, u32[]{:S(2)}, u32[]{:S(2)}) collective-permute-start(f32[16,64]{1,0:T(8,128)S(1)} %shard_map.121.b0), channel_id=1, source_target_pairs={{0,3},{1,0},{2,1},{3,2},{4,7},{5,4},{6,5},{7,6},{8,11},{9,8},{10,9... | collective-permute-start | bytes 12296 | tf_op jit(solution)/shard_map/ppermute | solution.py:235
  213.9 1.3 collective-permute-start.47
  215.2 2.2 shard_map.120
  218.0 0.7 shard_map.122
  (128 shorter events, 21.0 us)
Async XLA Ops:
  0.6 12.6 %collective-permute-start.3 = (f32[1024,1024]{1,0:T(8,128)}, f32[1024,1024]{1,0:T(8,128)}, u32[]{:S(2)}, u32[]{:S(2)}) collective-permute-start(f32[1024,1024]{1,0:T(8,128)} %bitcast.10), channel_id=1, source_target_pairs={{4,0},{12,8},{20,16},{28,24},{36,32},{44,40},{52,48},{60,56},{68,6... | collective-permute-start | bytes 12582920 | tf_op jit(solution)/shard_map/ppermute | solution.py:249
  9.6 1.5 collective-permute-start
  11.1 13.3 %collective-permute-start.1 = (f32[272,1024]{1,0:T(8,128)S(1)}, f32[272,1024]{1,0:T(8,128)S(1)}, u32[]{:S(2)}, u32[]{:S(2)}) collective-permute-start(f32[272,1024]{1,0:T(8,128)S(1)} %shard_map.86), channel_id=1, source_target_pairs={{8,0},{24,16},{40,32},{56,48},{72,64},{88,80},{104,96},{120,112},{... | collective-permute-start | bytes 3342344 | tf_op jit(solution)/shard_map/ppermute | solution.py:258
  11.8 4.5 %collective-permute-start.2 = (f32[16,1024]{1,0:T(8,128)S(1)}, f32[16,1024]{1,0:T(8,128)S(1)}, u32[]{:S(2)}, u32[]{:S(2)}) collective-permute-start(f32[16,1024]{1,0:T(8,128)S(1)} %dynamic-slice_bitcast_fusion.1.bias_ref.refs_5_.refs_7_), channel_id=1, source_target_pairs={{4,0},{12,8},{20,16},{28,24},{36,32},{44,40},{52,48},{60,56},{68,6... | collective-permute-start | bytes 196616 | tf_op jit(solution)/shard_map/ppermute | solution.py:250
  16.4 0.7 collective-permute-start.4
  17.1 0.7 collective-permute-start.5
  17.8 0.7 collective-permute-start.6
  18.5 0.7 collective-permute-start.7
  19.2 0.7 collective-permute-start.8
  20.0 0.7 collective-permute-start.9
  20.7 0.7 collective-permute-start.10
  21.4 0.7 collective-permute-start.11
  22.1 0.7 collective-permute-start.12
  24.5 0.9 collective-permute-start.15
  25.5 28.9 %collective-permute-start.16 = (f32[256,1024]{1,0:T(8,128)S(1)}, f32[256,1024]{1,0:T(8,128)S(1)}, u32[]{:S(2)}, u32[]{:S(2)}) collective-permute-start(f32[256,1024]{1,0:T(8,128)S(1)} %get-tuple-element.165.b0), channel_id=1, source_target_pairs={{16,17},{17,18},{18,19},{19,16},{40,41},{41,42},{42,43},{43,40},{4... | collective-permute-start | bytes 3145736 | tf_op jit(solution)/shard_map/ppermute | solution.py:235
  26.3 28.1 %collective-permute-start.17 = (f32[256,1024]{1,0:T(8,128)S(1)}, f32[256,1024]{1,0:T(8,128)S(1)}, u32[]{:S(2)}, u32[]{:S(2)}) collective-permute-start(f32[256,1024]{1,0:T(8,128)S(1)} %get-tuple-element.165.b0), channel_id=1, source_target_pairs={{16,19},{17,16},{18,17},{19,18},{40,43},{41,40},{42,41},{43,42},{4... | collective-permute-start | bytes 3145736 | tf_op jit(solution)/shard_map/ppermute | solution.py:235
  27.1 27.4 %collective-permute-start.18 = (f32[256,1024]{1,0:T(8,128)S(1)}, f32[256,1024]{1,0:T(8,128)S(1)}, u32[]{:S(2)}, u32[]{:S(2)}) collective-permute-start(f32[256,1024]{1,0:T(8,128)S(1)} %get-tuple-element.165.b0), channel_id=1, source_target_pairs={{16,18},{17,19},{18,16},{19,17},{40,42},{41,43},{42,40},{43,41},{4... | collective-permute-start | bytes 3145736 | tf_op jit(solution)/shard_map/ppermute | solution.py:235
  27.8 4.4 %collective-permute-start.19 = (f32[64,256]{1,0:T(8,128)S(1)}, f32[64,256]{1,0:T(8,128)S(1)}, u32[]{:S(2)}, u32[]{:S(2)}) collective-permute-start(f32[64,256]{1,0:T(8,128)S(1)} %bitcast.14), channel_id=1, source_target_pairs={{0,1},{1,2},{2,3},{3,0},{4,5},{5,6},{6,7},{7,4},{8,9},{9,10},{10,1... | collective-permute-start | bytes 196616 | tf_op jit(solution)/shard_map/ppermute | solution.py:235
  27.9 4.6 %collective-permute-start.20 = (f32[64,256]{1,0:T(8,128)S(1)}, f32[64,256]{1,0:T(8,128)S(1)}, u32[]{:S(2)}, u32[]{:S(2)}) collective-permute-start(f32[64,256]{1,0:T(8,128)S(1)} %bitcast.15), channel_id=1, source_target_pairs={{0,3},{1,0},{2,1},{3,2},{4,7},{5,4},{6,5},{7,6},{8,11},{9,8},{10,9... | collective-permute-start | bytes 196616 | tf_op jit(solution)/shard_map/ppermute | solution.py:235
  32.2 4.6 %collective-permute-start.21 = (f32[64,256]{1,0:T(8,128)S(1)}, f32[64,256]{1,0:T(8,128)S(1)}, u32[]{:S(2)}, u32[]{:S(2)}) collective-permute-start(f32[64,256]{1,0:T(8,128)S(1)} %bitcast.16), channel_id=1, source_target_pairs={{0,2},{1,3},{2,0},{3,1},{4,6},{5,7},{6,4},{7,5},{8,10},{9,11},{10,... | collective-permute-start | bytes 196616 | tf_op jit(solution)/shard_map/ppermute | solution.py:235
  36.9 17.5 %collective-permute-start.22 = (f32[64,1024]{1,0:T(8,128)S(1)}, f32[64,1024]{1,0:T(8,128)S(1)}, u32[]{:S(2)}, u32[]{:S(2)}) collective-permute-start(f32[64,1024]{1,0:T(8,128)S(1)} %shard_map.105.arrow_even), channel_id=1, source_target_pairs={{4,0},{12,8},{20,16},{28,24},{36,32},{44,40},{52,48},{60,56},{68,6... | collective-permute-start | bytes 786440 | tf_op jit(solution)/shard_map/ppermute | solution.py:287
  54.4 0.7 collective-permute-start.23
  61.1 1.4 collective-permute-start.32
  61.8 0.7 collective-permute-start.33
  63.5 108.5 %collective-permute-start.36 = (f32[32,1024]{1,0:T(8,128)S(1)}, f32[32,1024]{1,0:T(8,128)S(1)}, u32[]{:S(2)}, u32[]{:S(2)}) collective-permute-start(f32[32,1024]{1,0:T(8,128)S(1)} %get-tuple-element.199), channel_id=1, source_target_pairs={{0,4},{8,12},{16,20},{24,28},{32,36},{40,44},{48,52},{56,60},{64,6... | collective-permute-start | bytes 393224 | tf_op jit(solution)/shard_map/ppermute | solution.py:329
  172.0 5.1 %collective-permute-start.38 = (f32[32,1024]{1,0:T(8,128)S(1)}, f32[32,1024]{1,0:T(8,128)S(1)}, u32[]{:S(2)}, u32[]{:S(2)}) collective-permute-start(f32[32,1024]{1,0:T(8,128)S(1)} %shard_map.119.b0), channel_id=1, source_target_pairs={{0,1},{1,2},{2,3},{3,0},{4,5},{5,6},{6,7},{7,4},{8,9},{9,10},{10,1... | collective-permute-start | bytes 393224 | tf_op jit(solution)/shard_map/ppermute | solution.py:235
  172.2 5.9 %collective-permute-start.39 = (f32[32,1024]{1,0:T(8,128)S(1)}, f32[32,1024]{1,0:T(8,128)S(1)}, u32[]{:S(2)}, u32[]{:S(2)}) collective-permute-start(f32[32,1024]{1,0:T(8,128)S(1)} %shard_map.119.b0), channel_id=1, source_target_pairs={{0,3},{1,0},{2,1},{3,2},{4,7},{5,4},{6,5},{7,6},{8,11},{9,8},{10,9... | collective-permute-start | bytes 393224 | tf_op jit(solution)/shard_map/ppermute | solution.py:235
  174.8 5.3 %collective-permute-start.40 = (f32[32,1024]{1,0:T(8,128)S(1)}, f32[32,1024]{1,0:T(8,128)S(1)}, u32[]{:S(2)}, u32[]{:S(2)}) collective-permute-start(f32[32,1024]{1,0:T(8,128)S(1)} %shard_map.119.b0), channel_id=1, source_target_pairs={{0,2},{1,3},{2,0},{3,1},{4,6},{5,7},{6,4},{7,5},{8,10},{9,11},{10,... | collective-permute-start | bytes 393224 | tf_op jit(solution)/shard_map/ppermute | solution.py:235
  182.2 29.1 %collective-permute-start.44 = (f32[16,64]{1,0:T(8,128)S(1)}, f32[16,64]{1,0:T(8,128)S(1)}, u32[]{:S(2)}, u32[]{:S(2)}) collective-permute-start(f32[16,64]{1,0:T(8,128)S(1)} %add.27.keep_ref), channel_id=1, source_target_pairs={{0,4},{8,12},{16,20},{24,28},{32,36},{40,44},{48,52},{56,60},{64,6... | collective-permute-start | bytes 12296 | tf_op jit(solution)/shard_map/ppermute | solution.py:346
  211.3 6.1 %collective-permute-start.45 = (f32[16,64]{1,0:T(8,128)S(1)}, f32[16,64]{1,0:T(8,128)S(1)}, u32[]{:S(2)}, u32[]{:S(2)}) collective-permute-start(f32[16,64]{1,0:T(8,128)S(1)} %shard_map.121.b0), channel_id=1, source_target_pairs={{0,1},{1,2},{2,3},{3,0},{4,5},{5,6},{6,7},{7,4},{8,9},{9,10},{10,1... | collective-permute-start | bytes 12296 | tf_op jit(solution)/shard_map/ppermute | solution.py:235
  211.7 5.7 %collective-permute-start.46 = (f32[16,64]{1,0:T(8,128)S(1)}, f32[16,64]{1,0:T(8,128)S(1)}, u32[]{:S(2)}, u32[]{:S(2)}) collective-permute-start(f32[16,64]{1,0:T(8,128)S(1)} %shard_map.121.b0), channel_id=1, source_target_pairs={{0,3},{1,0},{2,1},{3,2},{4,7},{5,4},{6,5},{7,6},{8,11},{9,8},{10,9... | collective-permute-start | bytes 12296 | tf_op jit(solution)/shard_map/ppermute | solution.py:235
  213.9 4.0 %collective-permute-start.47 = (f32[16,64]{1,0:T(8,128)S(1)}, f32[16,64]{1,0:T(8,128)S(1)}, u32[]{:S(2)}, u32[]{:S(2)}) collective-permute-start(f32[16,64]{1,0:T(8,128)S(1)} %shard_map.121.b0), channel_id=1, source_target_pairs={{0,2},{1,3},{2,0},{3,1},{4,6},{5,7},{6,4},{7,5},{8,10},{9,11},{10,... | collective-permute-start | bytes 12296 | tf_op jit(solution)/shard_map/ppermute | solution.py:235
  (22 other events, 59.7 us)
